TPU v7x, 32 devices: a whole 2x2x4 slice. The times are simulated.
32 devices in a mesh: ctx: 8 (over y, x, core), chan: 4 (over z).
Axes of the slice: x: 2, y: 2, z: 4, core: 2. Of those that a mesh axis runs over, the one named last changes fastest.
Arguments:
- inputs: bfloat16 [256, 4096], P('ctx', 'chan'), may hold values from -6 to 6
- gain: float32 [4096], replicated, may hold values from 0.25 to 1.75
- w_in: bfloat16 [4096, 3, 4096], P(None, None, 'chan'), may hold values from -0.09375 to 0.09375
- w_out: bfloat16 [4096, 4096], P('chan'), may hold values from -0.125 to 0.125
- history: bfloat16 [2048, 2, 4096], P('ctx', None, 'chan'), may hold values from -6 to 6
- filt_far: bfloat16 [2048, 2, 4096], P('ctx', None, 'chan'), may hold values from -0.125 to 0.125
- filt_near: bfloat16 [256, 2, 4096], P(None, None, 'chan'), may hold values from -0.125 to 0.125
Outputs:
- mixed: bfloat16 [256, 4096], P('ctx', 'chan')
- gated: bfloat16 [256, 4096], P('ctx', 'chan')
All inputs are finite; a program needn't handle non-finite values.
Results may differ from a plain program's by a relative error of at most 0.0066.
Values may be sent and summed in bfloat16 or wider, within the bound.
A program may use at most 128 MiB of HBM per device.

v0:
```python
import jax
import jax.numpy as jnp
from jax import lax
from jax.sharding import PartitionSpec as P


def correlate(signal, kernel):
    result = lax.conv_general_dilated(
        signal[None],
        kernel[:, None, :],
        (1,),
        "VALID",
        dimension_numbers=("NWC", "WIO", "NWC"),
        feature_group_count=signal.shape[1],
        preferred_element_type=jnp.float32,
    )
    return result[0]


def per_device(inputs, gain, w_in, w_out, history, filt_far, filt_near):
    chan_width = inputs.shape[1]
    tok_rows = inputs.shape[0]
    fresh_count = filt_near.shape[0]
    ctx_index = lax.axis_index("ctx")
    ctx_count = lax.axis_size("ctx")
    gathered = lax.all_gather(inputs, "chan", axis=1, tiled=True)
    features = gathered.astype(jnp.float32)
    mean_sq = jnp.mean(features * features, axis=-1, keepdims=True)
    normed = (features * lax.rsqrt(mean_sq + 1e-06) * gain).astype(jnp.bfloat16)
    projected = jnp.dot(
        normed, w_in.reshape(w_in.shape[0], 3 * chan_width), preferred_element_type=jnp.float32
    )
    projected = projected.reshape(tok_rows, 3, chan_width)
    values = projected[:, 0].astype(jnp.bfloat16)
    gate_one = projected[:, 1].astype(jnp.bfloat16)
    gate_two = projected[:, 2].astype(jnp.bfloat16)
    column_count = chan_width // ctx_count
    hist_cols, far_cols = (
        lax.all_to_all(history, "ctx", split_axis=2, concat_axis=0, tiled=True),
        lax.all_to_all(filt_far, "ctx", split_axis=2, concat_axis=0, tiled=True),
    )
    value_cols, first_gate, second_gate = (
        lax.all_to_all(values, "ctx", split_axis=1, concat_axis=0, tiled=True),
        lax.all_to_all(gate_one, "ctx", split_axis=1, concat_axis=0, tiled=True),
        lax.all_to_all(gate_two, "ctx", split_axis=1, concat_axis=0, tiled=True),
    )
    near_cols = lax.dynamic_slice_in_dim(filt_near, ctx_index * column_count, column_count, 2)
    filter_rows = jnp.concatenate([far_cols, near_cols], 0)
    zero_tail = jnp.zeros((fresh_count - 1, column_count), jnp.bfloat16)

    def whole_conv(which, fresh_rows):
        signal = jnp.concatenate([filter_rows[:, which], zero_tail], 0)
        kernel = jnp.concatenate([hist_cols[:, which], fresh_rows], 0)
        return correlate(signal, kernel)[::-1]

    first_full = whole_conv(0, value_cols)
    gated_cols = (first_gate.astype(jnp.float32) * first_full).astype(jnp.bfloat16)
    second_full = whole_conv(1, gated_cols)
    mixed_cols = (second_gate.astype(jnp.float32) * second_full).astype(jnp.bfloat16)
    gated, mixed_in = (
        lax.all_to_all(gated_cols, "ctx", split_axis=0, concat_axis=1, tiled=True),
        lax.all_to_all(mixed_cols, "ctx", split_axis=0, concat_axis=1, tiled=True),
    )
    partial_out = jnp.dot(mixed_in, w_out, preferred_element_type=jnp.float32)
    mixed = lax.psum_scatter(partial_out, "chan", scatter_dimension=1, tiled=True).astype(
        jnp.bfloat16
    )
    return (mixed, gated)


def solution(mesh):
    placed = (
        P("ctx", "chan"),
        P(),
        P(None, None, "chan"),
        P("chan", None),
        P("ctx", None, "chan"),
        P("ctx", None, "chan"),
        P(None, None, "chan"),
    )
    return jax.shard_map(
        per_device,
        mesh=mesh,
        in_specs=placed,
        out_specs=(P("ctx", "chan"), P("ctx", "chan")),
        check_vma=False,
    )
```

profile of v0, /device:TPU:0, one launch (start us, length us, event | category | flops | bytes accessed | tf_op | source)
XLA Modules:
  0.0 247.2 jit_solution(8175190714699875306)
XLA Ops:
  7.2 5.0 %copy.59 = bf16[256,2,1024]{0,1,2:T(2,128)(2,1)} copy(bf16[256,2,1024]{2,1,0:T(2,128)(2,1)} %param.12) | data formatting | bytes 2097152 | tf_op args[5]
  12.2 5.2 %all-to-all-start.1 = ((bf16[256,2,1024]{0,1,2:T(2,128)(2,1)}), bf16[256,2,1024]{0,1,2:T(2,128)(2,1)S(1)}, u32[]{:S(2)}, u32[]{:S(2)}) async-start(bf16[256,2,1024]{0,1,2:T(2,128)(2,1)} %copy.59), calls=%async_computation.1 | async-start | bytes 2097152 | tf_op jit(solution)/shard_map/all_to_all | solution.py:40
  17.4 33.6 %copy.57 = bf16[4096,3,1024]{0,2,1:T(8,128)(2,1)} copy(bf16[4096,3,1024]{2,0,1:T(8,128)(2,1)} %param.9) | data formatting | bytes 50331648 | tf_op args[2]
  51.0 3.2 %copy.62 = bf16[256,2,1024]{0,1,2:T(2,128)(2,1)} copy(bf16[256,2,1024]{2,1,0:T(2,128)(2,1)S(1)} %copy-done.3) | data formatting | bytes 2097152 | tf_op args[4]
  54.2 14.2 %all_gather.3 = bf16[32,4096]{1,0:T(8,128)(2,1)S(1)} all-gather(bf16[32,1024]{1,0:T(8,128)(2,1)S(1)} %copy-done.4), channel_id=1, replica_groups=mesh['ctx'=8,'chan'=4] {'chan'}, dimensions={1}, use_global_device_ids=true | all-gather | bytes 327680 | tf_op jit(solution)/shard_map/all_gather | solution.py:26
  68.4 0.2 fusion.14
  68.6 0.6 copy-done.2
  69.1 4.1 %all-to-all-start.2 = ((bf16[256,2,1024]{0,1,2:T(2,128)(2,1)}), bf16[256,2,1024]{0,1,2:T(2,128)(2,1)S(1)}, u32[]{:S(2)}, u32[]{:S(2)}) async-start(bf16[256,2,1024]{0,1,2:T(2,128)(2,1)} %copy.62), calls=%async_computation.2 | async-start | bytes 2097152 | tf_op jit(solution)/shard_map/all_to_all | solution.py:39
  73.2 12.4 %fusion.8 = bf16[32,3,1024]{2,0,1:T(8,128)(2,1)S(1)} fusion(bf16[4096,3,1024]{0,2,1:T(8,128)(2,1)} %copy.57, bf16[32,4096]{1,0:T(8,128)(2,1)} %copy-done.2, f32[4096]{0:T(1024)S(1)} %copy-done.5, f32[32]{0:T(128)S(1)} %add_rsqrt_fusion), kind=kOutput, calls=%fused_computation.10 | convolution fusion | flops 805928960 | bytes 25641088 | tf_op jit(solution)/shard_map/dot_general | solution.py:30
  85.6 0.1 constant_dynamic-slice_fusion
  85.8 0.6 copy.65
  86.4 0.6 copy.64
  87.1 0.6 copy.58
  87.7 0.9 copy.60
  88.6 4.2 %all-to-all-start.4 = ((bf16[32,8,128]{2,0,1:T(8,128)(2,1)}), bf16[32,8,128]{2,0,1:T(8,128)(2,1)S(1)}, u32[]{:S(2)}, u32[]{:S(2)}) async-start(bf16[32,8,128]{2,0,1:T(8,128)(2,1)} %copy.65), calls=%async_computation.4 | async-start | bytes 131072 | tf_op jit(solution)/shard_map/all_to_all | solution.py:43
  92.8 0.9 copy.63
  93.7 0.1 slice_bitcast_fusion.1
  93.8 0.1 fusion.13
  93.9 3.9 %all-to-all-done.4 = bf16[32,8,128]{2,0,1:T(8,128)(2,1)S(1)} async-done(((bf16[32,8,128]{2,0,1:T(8,128)(2,1)}), bf16[32,8,128]{2,0,1:T(8,128)(2,1)S(1)}, u32[]{:S(2)}, u32[]{:S(2)}) %all-to-all-start.4) | async-done | bytes 65568 | tf_op jit(solution)/shard_map/all_to_all | solution.py:43
  97.8 3.4 %all-to-all-start.3 = ((bf16[32,8,128]{2,0,1:T(8,128)(2,1)}), bf16[32,8,128]{2,0,1:T(8,128)(2,1)S(1)}, u32[]{:S(2)}, u32[]{:S(2)}) async-start(bf16[32,8,128]{2,0,1:T(8,128)(2,1)} %copy.64), calls=%async_computation.3 | async-start | bytes 131072 | tf_op jit(solution)/shard_map/all_to_all | solution.py:44
  101.2 48.3 %fusion.4 = f32[1,256,128]{2,0,1:T(1,128)S(1)} fusion(bf16[1,2559,128]{2,1,0:T(8,128)(2,1)S(1)} %pad_bitcast_fusion, bf16[2304,1,128]{2,0,1:T(8,128)(2,1)S(1)} %maximum_bitcast_fusion), kind=kOutput, calls=%fused_computation.4 | convolution fusion | flops 150994944 | bytes 1376000 | tf_op jit(solution)/shard_map/conv_general_dilated | solution.py:8
  149.5 0.1 rev.6
  149.6 4.1 %all-to-all-start = ((bf16[32,8,128]{2,0,1:T(8,128)(2,1)}), bf16[32,8,128]{2,0,1:T(8,128)(2,1)S(1)}, u32[]{:S(2)}, u32[]{:S(2)}) async-start(bf16[32,8,128]{2,0,1:T(8,128)(2,1)} %copy.58), calls=%async_computation | async-start | bytes 131072 | tf_op jit(solution)/shard_map/all_to_all | solution.py:45
  153.8 0.2 reduce-scatter.2.cloned.1.call-start
  154.1 48.3 %fusion.2 = f32[1,256,128]{2,0,1:T(1,128)S(1)} fusion(bf16[1,2559,128]{2,1,0:T(8,128)(2,1)S(1)} %pad_bitcast_fusion.1, bf16[2304,1,128]{2,0,1:T(8,128)(2,1)S(1)} %maximum_bitcast_fusion.1), kind=kOutput, calls=%fused_computation.2 | convolution fusion | flops 150994944 | bytes 1376000 | tf_op jit(solution)/shard_map/conv_general_dilated | solution.py:8
  202.3 0.1 rev.7
  202.5 8.8 %all_to_all.110 = bf16[8,32,128]{2,1,0:T(8,128)(2,1)S(1)} all-to-all(bf16[8,32,128]{2,1,0:T(8,128)(2,1)S(1)} %bitcast.94), channel_id=1, replica_groups=mesh['ctx'=8,'chan'=4] {'ctx'}, dimensions={0} | all-to-all | bytes 131072 | tf_op jit(solution)/shard_map/all_to_all | solution.py:62
  211.2 5.8 %fusion.23 = f32[32,4096]{1,0:T(8,128)} fusion(bf16[1024,4096]{1,0:T(8,128)(2,1)} %param.10, bf16[8,32,128]{2,1,0:T(8,128)(2,1)S(1)} %all_to_all.110), kind=kOutput, calls=%fused_computation.34 | convolution fusion | flops 268435456 | bytes 8978432 | tf_op jit(solution)/shard_map/dot_general | solution.py:64
  217.1 7.4 %all_to_all.111 = bf16[8,32,128]{2,1,0:T(8,128)(2,1)S(1)} all-to-all(bf16[8,32,128]{2,1,0:T(8,128)(2,1)S(1)} %bitcast.89), channel_id=1, replica_groups=mesh['ctx'=8,'chan'=4] {'ctx'}, dimensions={0} | all-to-all | bytes 131072 | tf_op jit(solution)/shard_map/all_to_all | solution.py:61
  224.5 0.6 copy_bitcast_fusion
  225.1 13.7 %reduce-scatter.2.cloned.1.call-done = f32[32,1024]{1,0:T(8,128)} async-done(((f32[32,4096]{1,0:T(8,128)}), f32[32,1024]{1,0:T(8,128)}) %reduce-scatter.2.cloned.1.call-update) | async-done | bytes 131088 | tf_op jit(solution)/shard_map/reduce_scatter | solution.py:65
  238.8 1.5 convert_element_type.61
  (28 shorter events, 0.3 us)
Async XLA Ops:
  7.2 78.4 %copy-start = (bf16[256,2,1024]{2,1,0:T(2,128)(2,1)S(1)}, bf16[256,2,1024]{2,1,0:T(2,128)(2,1)}, u32[]{:S(2)}) copy-start(bf16[256,2,1024]{2,1,0:T(2,128)(2,1)} %param.13) | copy-start | bytes 3145732
  12.2 57.0 %all-to-all-start.1 = ((bf16[256,2,1024]{0,1,2:T(2,128)(2,1)}), bf16[256,2,1024]{0,1,2:T(2,128)(2,1)S(1)}, u32[]{:S(2)}, u32[]{:S(2)}) async-start(bf16[256,2,1024]{0,1,2:T(2,128)(2,1)} %copy.59), calls=%async_computation.1 | async-start | bytes 2097152 | tf_op jit(solution)/shard_map/all_to_all | solution.py:40
  17.4 33.6 %copy-start.3 = (bf16[256,2,1024]{2,1,0:T(2,128)(2,1)S(1)}, bf16[256,2,1024]{2,1,0:T(2,128)(2,1)}, u32[]{:S(2)}) copy-start(bf16[256,2,1024]{2,1,0:T(2,128)(2,1)} %param.11) | copy-start | bytes 3145732
  51.0 3.2 %copy-start.4 = (bf16[32,1024]{1,0:T(8,128)(2,1)S(1)}, bf16[32,1024]{1,0:T(8,128)(2,1)}, u32[]{:S(2)}) copy-start(bf16[32,1024]{1,0:T(8,128)(2,1)} %param.7) | copy-start | bytes 196612
  68.4 0.7 copy-start.2
  68.4 4.8 %copy-start.5 = (f32[4096]{0:T(1024)S(1)}, f32[4096]{0:T(1024)}, u32[]{:S(2)}) copy-start(f32[4096]{0:T(1024)} %param.8) | copy-start | bytes 49156
  69.1 19.5 %all-to-all-start.2 = ((bf16[256,2,1024]{0,1,2:T(2,128)(2,1)}), bf16[256,2,1024]{0,1,2:T(2,128)(2,1)S(1)}, u32[]{:S(2)}, u32[]{:S(2)}) async-start(bf16[256,2,1024]{0,1,2:T(2,128)(2,1)} %copy.62), calls=%async_computation.2 | async-start | bytes 2097152 | tf_op jit(solution)/shard_map/all_to_all | solution.py:39
  88.6 9.2 %all-to-all-start.4 = ((bf16[32,8,128]{2,0,1:T(8,128)(2,1)}), bf16[32,8,128]{2,0,1:T(8,128)(2,1)S(1)}, u32[]{:S(2)}, u32[]{:S(2)}) async-start(bf16[32,8,128]{2,0,1:T(8,128)(2,1)} %copy.65), calls=%async_computation.4 | async-start | bytes 131072 | tf_op jit(solution)/shard_map/all_to_all | solution.py:43
  97.8 51.8 %all-to-all-start.3 = ((bf16[32,8,128]{2,0,1:T(8,128)(2,1)}), bf16[32,8,128]{2,0,1:T(8,128)(2,1)S(1)}, u32[]{:S(2)}, u32[]{:S(2)}) async-start(bf16[32,8,128]{2,0,1:T(8,128)(2,1)} %copy.64), calls=%async_computation.3 | async-start | bytes 131072 | tf_op jit(solution)/shard_map/all_to_all | solution.py:44
  149.6 52.8 %all-to-all-start = ((bf16[32,8,128]{2,0,1:T(8,128)(2,1)}), bf16[32,8,128]{2,0,1:T(8,128)(2,1)S(1)}, u32[]{:S(2)}, u32[]{:S(2)}) async-start(bf16[32,8,128]{2,0,1:T(8,128)(2,1)} %copy.58), calls=%async_computation | async-start | bytes 131072 | tf_op jit(solution)/shard_map/all_to_all | solution.py:45
  153.8 85.0 %reduce-scatter.2.cloned.1.call-start = ((), (), s32[]{:S(2)}) async-start(), calls=%async_computation.8 | async-start | bytes 655360 | tf_op jit(solution)/shard_map/reduce_scatter | solution.py:65
  211.2 29.1 %copy-start.1 = (bf16[256,2,1024]{2,1,0:T(2,128)(2,1)S(1)}, bf16[256,2,1024]{2,1,0:T(2,128)(2,1)}, u32[]{:S(2)}) copy-start(bf16[256,2,1024]{2,1,0:T(2,128)(2,1)} %param.13) | copy-start | bytes 3145732
Sparse Core Ops, SparseCore 0:
  217.2 21.5 reduce-scatter.1
where the time goes:
time: 249 us; the launch traced here: 247 us
  matrix products  115 us (46%)
  local copies, waits for them, and re-layouts  47.2 us (19%)
  blocking collectives  30.4 us (12%)
  starting transfers between devices  21.1 us (8%)
  waiting for transfers between devices  17.6 us (7%)
  between operations  14.3 us (6%)
    conv_general_dilated x2, matrix products, correlate(): lax.conv_general_dilated(signal[None], kernel[:, None, :], (1,), 'VALID',...  96.5 us
    unnamed x20, local copies, waits for them, and re-layouts  42.4 us
    all_gather x1, blocking collectives, per_device(): gathered = lax.all_gather(inputs, 'chan', axis=1, tiled=True)  14.2 us
    reduce_scatter x1, waiting for transfers between devices, per_device(): lax.psum_scatter(partial_out, 'chan', scatter_dimension=1, tiled=True)  13.7 us
    dot_general x1, matrix products, per_device(): jnp.dot(normed, w_in.reshape(w_in.shape[0], 3 * chan_width), preferred_el...  12.4 us
    all_to_all x1, blocking collectives, per_device(): lax.all_to_all(mixed_cols, 'ctx', split_axis=0, concat_axis=1, tiled=True)  8.79 us
    all_to_all x1, blocking collectives, per_device(): lax.all_to_all(gated_cols, 'ctx', split_axis=0, concat_axis=1, tiled=True)  7.4 us
    dot_general x1, matrix products, per_device(): partial_out = jnp.dot(mixed_in, w_out, preferred_element_type=jnp.float32)  5.84 us
  transfers between devices with their start and end apart: 6, of which 2 were waited for; matrix products, arithmetic and copies ran while one was open for 61% of the time, Pallas kernels for 0%

commit v1 on v0

v1 whole, which is shorter than its diff:
```python
import jax
import jax.numpy as jnp
import numpy as np
from jax import lax
from jax.sharding import PartitionSpec as P


def split_pair(matrix):
    high = matrix.astype(jnp.bfloat16)
    low = (matrix - high.astype(np.float64)).astype(jnp.bfloat16)
    return high, low


def transforms(block):
    angle = np.pi * (np.arange(block)[:, None] + 0.5) * np.arange(block)[None, :] / block
    forward = np.concatenate([np.cos(angle), -np.sin(angle)], 0)
    inverse = np.concatenate([np.cos(angle), -np.sin(angle)], 0).T[::-1] / block
    sign = np.where(np.arange(block) % 2 == 0, 1.0, -1.0).astype(np.float32)
    return split_pair(forward), split_pair(inverse), sign


def times(a, b):
    return jnp.dot(a, b, preferred_element_type=jnp.float32)


def per_device(inputs, gain, w_in, w_out, history, filt_far, filt_near):
    chan_width = inputs.shape[1]
    block = filt_near.shape[0]
    ctx_index = lax.axis_index("ctx")
    ctx_count = lax.axis_size("ctx")
    column_count = chan_width // ctx_count
    (fwd_hi, fwd_lo), (inv_hi, inv_lo), sign = transforms(block)
    sign = jnp.asarray(sign)[None, :, None]

    gathered = lax.all_gather(inputs, "chan", axis=1, tiled=True)
    features = gathered.astype(jnp.float32)
    mean_sq = jnp.mean(features * features, axis=-1, keepdims=True)
    normed = (features * lax.rsqrt(mean_sq + 1e-06) * gain).astype(jnp.bfloat16)
    weights = w_in.transpose(1, 0, 2)
    fresh = [
        lax.all_to_all(
            times(normed, weights[i]).astype(jnp.bfloat16),
            "ctx",
            split_axis=1,
            concat_axis=0,
            tiled=True,
        )
        for i in range(3)
    ]
    value_cols, first_gate, second_gate = fresh
    hist_cols, far_cols = (
        lax.all_to_all(history, "ctx", split_axis=2, concat_axis=0, tiled=True),
        lax.all_to_all(filt_far, "ctx", split_axis=2, concat_axis=0, tiled=True),
    )
    near_cols = lax.dynamic_slice_in_dim(filt_near, ctx_index * column_count, column_count, 2)
    old_blocks = hist_cols.shape[0] // block

    def forward(rows):
        return times(fwd_hi, rows) + times(fwd_lo, rows)

    def as_columns(rows):
        count = rows.shape[0] // block
        return (
            rows.reshape(count, block, 2, column_count)
            .transpose(1, 2, 0, 3)
            .reshape(block, 2 * count * column_count)
        )

    def as_spectra(freq, count):
        return freq.reshape(2, block, 2, count, column_count).transpose(3, 0, 1, 2, 4)

    hist_f = as_spectra(forward(as_columns(hist_cols)), old_blocks)
    far_f = as_spectra(forward(as_columns(far_cols)), old_blocks)
    near_f = as_spectra(forward(as_columns(near_cols)), 1)
    filt_f = jnp.concatenate([far_f, near_f], 0)
    tap_re, tap_im = filt_f[:, 0], filt_f[:, 1]
    turn = jnp.asarray(sign)[..., None]
    win_re = tap_re[:-1] + turn * tap_im[1:]
    win_im = tap_im[:-1] - turn * tap_re[1:]
    old_re, old_im = hist_f[:, 0], hist_f[:, 1]
    sum_re = jnp.sum(win_re * old_re + win_im * old_im, 0)
    sum_im = jnp.sum(win_im * old_re - win_re * old_im, 0)

    def whole_conv(which, rows):
        new_f = forward(rows)
        new_re, new_im = new_f[:block], new_f[block:]
        near_re, near_im = near_f[0, 0, :, which], near_f[0, 1, :, which]
        total = jnp.concatenate(
            [
                sum_re[:, which] + near_re * new_re + near_im * new_im,
                sum_im[:, which] + near_im * new_re - near_re * new_im,
            ],
            0,
        )
        high = lax.reduce_precision(total, 8, 7)
        low = (total - high).astype(jnp.bfloat16)
        high = high.astype(jnp.bfloat16)
        return times(inv_hi, high) + times(inv_lo, high) + times(inv_hi, low)

    first_full = whole_conv(0, value_cols)
    gated_cols = (first_gate.astype(jnp.float32) * first_full).astype(jnp.bfloat16)
    second_full = whole_conv(1, gated_cols)
    mixed_cols = (second_gate.astype(jnp.float32) * second_full).astype(jnp.bfloat16)
    gated, mixed_in = (
        lax.all_to_all(gated_cols, "ctx", split_axis=0, concat_axis=1, tiled=True),
        lax.all_to_all(mixed_cols, "ctx", split_axis=0, concat_axis=1, tiled=True),
    )
    partial_out = jnp.dot(mixed_in, w_out, preferred_element_type=jnp.float32)
    mixed = lax.psum_scatter(partial_out, "chan", scatter_dimension=1, tiled=True).astype(
        jnp.bfloat16
    )
    return (mixed, gated)


def solution(mesh):
    placed = (
        P("ctx", "chan"),
        P(),
        P(None, None, "chan"),
        P("chan", None),
        P("ctx", None, "chan"),
        P("ctx", None, "chan"),
        P(None, None, "chan"),
    )
    return jax.shard_map(
        per_device,
        mesh=mesh,
        in_specs=placed,
        out_specs=(P("ctx", "chan"), P("ctx", "chan")),
        check_vma=False,
    )
```

time: 249 us -> 150 us (0.60)
  matrix products: 115 us -> 29.2 us
  local copies, waits for them, and re-layouts: 47.2 us -> 22.4 us
  waiting for transfers between devices: 17.6 us -> 27.4 us
  other arithmetic: 1.91 us -> 5.08 us
    conv_general_dilated x2 -> x0, matrix products: 96.5 us -> none  [correlate(): lax.conv_general_dilated(signal[None], kernel[:, None, :], (1,), 'VALID',...]
    unnamed x20 -> x40, local copies, waits for them, and re-layouts: 42.4 us -> 15.3 us
    dot_general x1 -> x19, matrix products: 12.4 us -> 23.4 us  [times(): return jnp.dot(a, b, preferred_element_type=jnp.float32)]
    all_to_all x1, waiting for transfers between devices: 0.01 us -> 8.69 us  [per_device(): lax.all_to_all(history, 'ctx', split_axis=2, concat_axis=0, tiled=True)]
    all_to_all x1, waiting for transfers between devices: 0.01 us -> 5.15 us  [per_device(): lax.all_to_all(filt_far, 'ctx', split_axis=2, concat_axis=0, tiled=True)]
    all_to_all x3, waiting for transfers between devices: 3.91 us -> 0.02 us  [per_device(): lax.all_to_all(times(normed, weights[i]).astype(jnp.bfloat16), 'ctx', spl...]
  transfers between devices with their start and end apart: 6 -> 6, of which waited for: 2 -> 3; matrix products, arithmetic and copies ran while one was open for 61% -> 22% of each run, Pallas kernels for 0% -> 0%
where the time goes in v1:
time: 150 us; the launch traced here: 149 us
  blocking collectives  30.8 us (21%)
  matrix products  29.2 us (19%)
  waiting for transfers between devices  27.4 us (18%)
  local copies, waits for them, and re-layouts  22.4 us (15%)
  starting transfers between devices  20.1 us (13%)
  between operations  14.5 us (10%)
  other arithmetic  5.08 us (3%)
    dot_general x19, matrix products, times(): return jnp.dot(a, b, preferred_element_type=jnp.float32)  23.4 us
    all_gather x1, blocking collectives, per_device(): gathered = lax.all_gather(inputs, 'chan', axis=1, tiled=True)  16 us
    unnamed x40, local copies, waits for them, and re-layouts  15.3 us
    reduce_scatter x1, waiting for transfers between devices, per_device(): lax.psum_scatter(partial_out, 'chan', scatter_dimension=1, tiled=True)  13.5 us
    all_to_all x3, starting transfers between devices, per_device(): lax.all_to_all(times(normed, weights[i]).astype(jnp.bfloat16), 'ctx', spl...  12.1 us
    all_to_all x1, waiting for transfers between devices, per_device(): lax.all_to_all(history, 'ctx', split_axis=2, concat_axis=0, tiled=True)  8.69 us
    all_to_all x1, blocking collectives, per_device(): lax.all_to_all(mixed_cols, 'ctx', split_axis=0, concat_axis=1, tiled=True)  7.4 us
    all_to_all x1, blocking collectives, per_device(): lax.all_to_all(gated_cols, 'ctx', split_axis=0, concat_axis=1, tiled=True)  7.4 us
  transfers between devices with their start and end apart: 6, of which 3 were waited for; matrix products, arithmetic and copies ran while one was open for 22% of the time, Pallas kernels for 0%

profile of v1, /device:TPU:0, one launch (start us, length us, event | category | flops | bytes accessed | tf_op | source)
XLA Modules:
  0.0 149.4 jit_solution(18429281724813846505)
XLA Ops:
  7.2 16.0 %all_gather.3 = bf16[32,4096]{1,0:T(8,128)(2,1)S(1)} all-gather(bf16[32,1024]{1,0:T(8,128)(2,1)} %param.12), channel_id=1, replica_groups=mesh['ctx'=8,'chan'=4] {'chan'}, dimensions={1}, use_global_device_ids=true | all-gather | bytes 327680 | tf_op jit(solution)/shard_map/all_gather | solution.py:35
  23.4 5.0 %fusion.20 = bf16[4,8,8,128]{3,2,1,0:T(8,128)(2,1)S(1)} fusion(bf16[3,4096,1024]{2,1,0:T(8,128)(2,1)} %bitcast.211, bf16[32,4096]{1,0:T(8,128)(2,1)S(1)} %all_gather.3, f32[4096]{0:T(1024)} %param.13, f32[32]{0:T(128)S(1)} %add_rsqrt_fusion), kind=kOutput, calls=%fused_computation.40 | convolution fusion | flops 268992512 | bytes 8732800 | tf_op jit(solution)/shard_map/dot_general | solution.py:23
  29.0 3.7 %all-to-all-start.4 = ((bf16[32,8,128]{2,0,1:T(8,128)(2,1)}), bf16[32,8,128]{2,0,1:T(8,128)(2,1)S(1)}, u32[]{:S(2)}, u32[]{:S(2)}) async-start(bf16[32,8,128]{2,0,1:T(8,128)(2,1)} %bitcast.196), calls=%async_computation.4 | async-start | bytes 131072 | tf_op jit(solution)/shard_map/all_to_all | solution.py:41
  32.8 5.0 %fusion.21 = bf16[4,8,8,128]{3,2,1,0:T(8,128)(2,1)S(1)} fusion(bf16[3,4096,1024]{2,1,0:T(8,128)(2,1)} %bitcast.212, bf16[32,4096]{1,0:T(8,128)(2,1)S(1)} %all_gather.3, f32[4096]{0:T(1024)S(1)} %copy-done.15, f32[32]{0:T(128)S(1)} %add_rsqrt_fusion), kind=kOutput, calls=%fused_computation.41 | convolution fusion | flops 268992512 | bytes 8732800 | tf_op jit(solution)/shard_map/dot_general | solution.py:23
  38.4 4.2 %all-to-all-start.3 = ((bf16[32,8,128]{2,0,1:T(8,128)(2,1)}), bf16[32,8,128]{2,0,1:T(8,128)(2,1)S(1)}, u32[]{:S(2)}, u32[]{:S(2)}) async-start(bf16[32,8,128]{2,0,1:T(8,128)(2,1)} %bitcast.197), calls=%async_computation.3 | async-start | bytes 131072 | tf_op jit(solution)/shard_map/all_to_all | solution.py:41
  42.6 5.0 %fusion.22 = bf16[4,8,8,128]{3,2,1,0:T(8,128)(2,1)S(1)} fusion(bf16[3,4096,1024]{2,1,0:T(8,128)(2,1)} %bitcast.213, bf16[32,4096]{1,0:T(8,128)(2,1)S(1)} %all_gather.3, f32[4096]{0:T(1024)S(1)} %copy-done.15, f32[32]{0:T(128)S(1)} %add_rsqrt_fusion), kind=kOutput, calls=%fused_computation.42 | convolution fusion | flops 268992512 | bytes 8732800 | tf_op jit(solution)/shard_map/dot_general | solution.py:23
  48.2 4.2 %all-to-all-start = ((bf16[32,8,128]{2,0,1:T(8,128)(2,1)}), bf16[32,8,128]{2,0,1:T(8,128)(2,1)S(1)}, u32[]{:S(2)}, u32[]{:S(2)}) async-start(bf16[32,8,128]{2,0,1:T(8,128)(2,1)} %bitcast.198), calls=%async_computation | async-start | bytes 131072 | tf_op jit(solution)/shard_map/all_to_all | solution.py:41
  52.6 4.9 %copy.91 = bf16[256,2,1024]{0,1,2:T(2,128)(2,1)} copy(bf16[256,2,1024]{2,1,0:T(2,128)(2,1)} %param.17) | data formatting | bytes 2097152 | tf_op args[5]
  57.5 4.2 %all-to-all-start.1 = ((bf16[256,2,1024]{0,1,2:T(2,128)(2,1)}), bf16[256,2,1024]{0,1,2:T(2,128)(2,1)S(1)}, u32[]{:S(2)}, u32[]{:S(2)}) async-start(bf16[256,2,1024]{0,1,2:T(2,128)(2,1)} %copy.91), calls=%async_computation.1 | async-start | bytes 2097152 | tf_op jit(solution)/shard_map/all_to_all | solution.py:53
  63.1 4.9 %copy.94 = bf16[256,2,1024]{0,1,2:T(2,128)(2,1)} copy(bf16[256,2,1024]{2,1,0:T(2,128)(2,1)} %param.16) | data formatting | bytes 2097152 | tf_op args[4]
  68.0 1.2 fusion.58
  69.2 0.8 copy.105
  69.9 0.8 copy.108
  70.7 1.2 fusion.43
  71.9 5.1 %all-to-all-done.1 = bf16[256,2,1024]{0,1,2:T(2,128)(2,1)S(1)} async-done(((bf16[256,2,1024]{0,1,2:T(2,128)(2,1)}), bf16[256,2,1024]{0,1,2:T(2,128)(2,1)S(1)}, u32[]{:S(2)}, u32[]{:S(2)}) %all-to-all-start.1) | async-done | bytes 1048608 | tf_op jit(solution)/shard_map/all_to_all | solution.py:53
  77.0 3.6 %all-to-all-start.2 = ((bf16[256,2,1024]{0,1,2:T(2,128)(2,1)}), bf16[256,2,1024]{0,1,2:T(2,128)(2,1)S(1)}, u32[]{:S(2)}, u32[]{:S(2)}) async-start(bf16[256,2,1024]{0,1,2:T(2,128)(2,1)} %copy.94), calls=%async_computation.2 | async-start | bytes 2097152 | tf_op jit(solution)/shard_map/all_to_all | solution.py:52
  80.8 1.9 %fusion.10 = f32[512,128]{0,1:T(8,128)} fusion(f32[128,512]{1,0:T(8,128)S(1)} %fusion.43, bf16[512,256]{1,0:T(8,128)(2,1)} %constant.39, bf16[32,8,128]{2,0,1:T(8,128)(2,1)S(1)} %all-to-all-done.4), kind=kOutput, calls=%fused_computation.26 | convolution fusion | flops 33619968 | bytes 851968 | tf_op jit(solution)/shard_map/dot_general | solution.py:23
  82.8 0.7 fusion.61
  83.6 0.8 add_bitcast_fusion.1
  84.4 2.8 %copy.126 = f32[64,8,16,128]{3,2,1,0:T(8,128)} copy(f32[64,8,16,128]{3,1,2,0:T(8,128)S(1)} %add_bitcast_fusion.1) | data formatting | bytes 8388608
  87.2 8.7 %all-to-all-done.2 = bf16[256,2,1024]{0,1,2:T(2,128)(2,1)S(1)} async-done(((bf16[256,2,1024]{0,1,2:T(2,128)(2,1)}), bf16[256,2,1024]{0,1,2:T(2,128)(2,1)S(1)}, u32[]{:S(2)}, u32[]{:S(2)}) %all-to-all-start.2) | async-done | bytes 1048608 | tf_op jit(solution)/shard_map/all_to_all | solution.py:52
  96.0 0.7 fusion.62
  96.8 0.8 add_bitcast_fusion
  97.6 0.9 copy.128
  98.6 1.2 copy-done.2
  99.8 1.4 fusion.7
  101.3 1.8 %add_reduce_fusion = (f32[256,2,128]{2,1,0:T(2,128)S(1)}, f32[256,2,128]{2,1,0:T(2,128)S(1)}) fusion(f32[8,256,2,128]{3,0,2,1:T(8,128)S(1)} %get-tuple-element.5, f32[8,256,2,128]{3,0,2,1:T(8,128)S(1)} %get-tuple-element.4, f32[8,2,256,2,128]{4,0,3,2,1:T(8,128)S(1)} %bitcast.200), kind=kLoop, calls=%fused_computation.20 | loop fusion | flops 4063232 | bytes 8912896 | tf_op jit(solution)/shard_map/reduce_sum | solution.py:81
  106.2 7.4 %all_to_all.101 = bf16[8,32,128]{2,1,0:T(8,128)(2,1)S(1)} all-to-all(bf16[8,32,128]{2,1,0:T(8,128)(2,1)S(1)} %bitcast.209), channel_id=1, replica_groups=mesh['ctx'=8,'chan'=4] {'ctx'}, dimensions={0} | all-to-all | bytes 131072 | tf_op jit(solution)/shard_map/all_to_all | solution.py:106
  113.6 5.8 %fusion.39 = f32[32,4096]{1,0:T(8,128)} fusion(bf16[1024,4096]{1,0:T(8,128)(2,1)} %param.15, bf16[8,32,128]{2,1,0:T(8,128)(2,1)S(1)} %all_to_all.101), kind=kOutput, calls=%fused_computation.74 | convolution fusion | flops 268435456 | bytes 8978432 | tf_op jit(solution)/shard_map/dot_general | solution.py:108
  119.5 7.4 %all_to_all.102 = bf16[8,32,128]{2,1,0:T(8,128)(2,1)S(1)} all-to-all(bf16[8,32,128]{2,1,0:T(8,128)(2,1)S(1)} %bitcast.210), channel_id=1, replica_groups=mesh['ctx'=8,'chan'=4] {'ctx'}, dimensions={0} | all-to-all | bytes 131072 | tf_op jit(solution)/shard_map/all_to_all | solution.py:105
  127.6 13.5 %reduce-scatter.2.cloned.1.call-done = f32[32,1024]{1,0:T(8,128)} async-done(((f32[32,4096]{1,0:T(8,128)}), f32[32,1024]{1,0:T(8,128)}) %reduce-scatter.2.cloned.1.call-update) | async-done | bytes 131088 | tf_op jit(solution)/shard_map/reduce_scatter | solution.py:109
  141.0 1.5 %convert_element_type.71 = bf16[32,1024]{1,0:T(8,128)(2,1)} convert(f32[32,1024]{1,0:T(8,128)} %reduce-scatter.2.cloned.1.call-done) | non-fusion elementwise | flops 32768 | bytes 196608 | tf_op jit(solution)/shard_map/convert_element_type | solution.py:109
  (68 shorter events, 7.8 us)
Async XLA Ops:
  7.2 45.3 %copy-start = (bf16[256,2,1024]{2,1,0:T(2,128)(2,1)S(1)}, bf16[256,2,1024]{2,1,0:T(2,128)(2,1)}, u32[]{:S(2)}) copy-start(bf16[256,2,1024]{2,1,0:T(2,128)(2,1)} %param.18) | copy-start | bytes 3145732
  23.4 9.4 %copy-start.15 = (f32[4096]{0:T(1024)S(1)}, f32[4096]{0:T(1024)}, u32[]{:S(2)}) copy-start(f32[4096]{0:T(1024)} %param.13) | copy-start | bytes 49156
  29.0 9.4 %all-to-all-start.4 = ((bf16[32,8,128]{2,0,1:T(8,128)(2,1)}), bf16[32,8,128]{2,0,1:T(8,128)(2,1)S(1)}, u32[]{:S(2)}, u32[]{:S(2)}) async-start(bf16[32,8,128]{2,0,1:T(8,128)(2,1)} %bitcast.196), calls=%async_computation.4 | async-start | bytes 131072 | tf_op jit(solution)/shard_map/all_to_all | solution.py:41
  38.4 9.8 %all-to-all-start.3 = ((bf16[32,8,128]{2,0,1:T(8,128)(2,1)}), bf16[32,8,128]{2,0,1:T(8,128)(2,1)S(1)}, u32[]{:S(2)}, u32[]{:S(2)}) async-start(bf16[32,8,128]{2,0,1:T(8,128)(2,1)} %bitcast.197), calls=%async_computation.3 | async-start | bytes 131072 | tf_op jit(solution)/shard_map/all_to_all | solution.py:41
  47.6 14.1 %copy-start.5 = (bf16[512,256]{1,0:T(8,128)(2,1)S(1)}, bf16[512,256]{1,0:T(8,128)(2,1)}, u32[]{:S(2)}) copy-start(bf16[512,256]{1,0:T(8,128)(2,1)} %constant.30.clone) | copy-start | bytes 786436
  47.6 14.3 %copy-start.3 = (bf16[512,256]{1,0:T(8,128)(2,1)S(1)}, bf16[512,256]{1,0:T(8,128)(2,1)}, u32[]{:S(2)}) copy-start(bf16[512,256]{1,0:T(8,128)(2,1)} %constant.31.clone) | copy-start | bytes 786436
  48.2 9.2 %all-to-all-start = ((bf16[32,8,128]{2,0,1:T(8,128)(2,1)}), bf16[32,8,128]{2,0,1:T(8,128)(2,1)S(1)}, u32[]{:S(2)}, u32[]{:S(2)}) async-start(bf16[32,8,128]{2,0,1:T(8,128)(2,1)} %bitcast.198), calls=%async_computation | async-start | bytes 131072 | tf_op jit(solution)/shard_map/all_to_all | solution.py:41
  57.5 19.6 %all-to-all-start.1 = ((bf16[256,2,1024]{0,1,2:T(2,128)(2,1)}), bf16[256,2,1024]{0,1,2:T(2,128)(2,1)S(1)}, u32[]{:S(2)}, u32[]{:S(2)}) async-start(bf16[256,2,1024]{0,1,2:T(2,128)(2,1)} %copy.91), calls=%async_computation.1 | async-start | bytes 2097152 | tf_op jit(solution)/shard_map/all_to_all | solution.py:53
  77.0 18.9 %all-to-all-start.2 = ((bf16[256,2,1024]{0,1,2:T(2,128)(2,1)}), bf16[256,2,1024]{0,1,2:T(2,128)(2,1)S(1)}, u32[]{:S(2)}, u32[]{:S(2)}) async-start(bf16[256,2,1024]{0,1,2:T(2,128)(2,1)} %copy.94), calls=%async_computation.2 | async-start | bytes 2097152 | tf_op jit(solution)/shard_map/all_to_all | solution.py:52
  80.6 60.5 %reduce-scatter.2.cloned.1.call-start = ((), (), s32[]{:S(2)}) async-start(), calls=%async_computation.8 | async-start | bytes 655360 | tf_op jit(solution)/shard_map/reduce_scatter | solution.py:109
  97.6 2.2 %copy-start.2 = (f32[64,8,16,128]{3,2,1,0:T(8,128)S(1)}, f32[64,8,16,128]{3,2,1,0:T(8,128)}, u32[]{:S(2)}) copy-start(f32[64,8,16,128]{3,2,1,0:T(8,128)} %copy.126) | copy-start | bytes 12582916
  97.6 2.2 %copy-start.14 = (f32[256]{0:T(256)S(1)}, f32[256]{0:T(256)}, u32[]{:S(2)}) copy-start(f32[256]{0:T(256)} %constant.29.clone) | copy-start | bytes 3076
  101.3 2.5 %copy-start.7 = (f32[512,128]{0,1:T(8,128)S(1)}, f32[512,128]{0,1:T(8,128)}, u32[]{:S(2)}) copy-start(f32[512,128]{0,1:T(8,128)} %fusion.10) | copy-start | bytes 786436
  101.3 2.5 %copy-start.12 = (f32[1,1,256,1,128]{2,1,4,3,0:T(1,128)S(1)}, f32[1,1,256,1,128]{2,1,4,3,0:T(1,128)}, u32[]{:S(2)}) copy-start(f32[1,1,256,1,128]{2,1,4,3,0:T(1,128)} %get-tuple-element.10) | copy-start | bytes 393220
  101.3 2.5 %copy-start.13 = (f32[1,1,256,1,128]{2,1,4,3,0:T(1,128)S(1)}, f32[1,1,256,1,128]{2,1,4,3,0:T(1,128)}, u32[]{:S(2)}) copy-start(f32[1,1,256,1,128]{2,1,4,3,0:T(1,128)} %get-tuple-element.11) | copy-start | bytes 393220
  101.3 2.6 %copy-start.4 = (bf16[256,512]{1,0:T(8,128)(2,1)S(1)}, bf16[256,512]{1,0:T(8,128)(2,1)}, u32[]{:S(2)}) copy-start(bf16[256,512]{1,0:T(8,128)(2,1)} %constant.32.clone) | copy-start | bytes 786436
  101.3 2.8 %copy-start.6 = (bf16[256,512]{1,0:T(8,128)(2,1)S(1)}, bf16[256,512]{1,0:T(8,128)(2,1)}, u32[]{:S(2)}) copy-start(bf16[256,512]{1,0:T(8,128)(2,1)} %constant.33.clone) | copy-start | bytes 786436
  101.3 3.0 %copy-start.9 = (f32[256,128]{0,1:T(8,128)S(1)}, f32[256,128]{0,1:T(8,128)}, u32[]{:S(2)}) copy-start(f32[256,128]{0,1:T(8,128)} %copy.105) | copy-start | bytes 393220
  103.1 2.1 %copy-start.10 = (f32[1,1,256,1,128]{2,1,4,3,0:T(1,128)S(1)}, f32[1,1,256,1,128]{2,1,4,3,0:T(1,128)}, u32[]{:S(2)}) copy-start(f32[1,1,256,1,128]{2,1,4,3,0:T(1,128)} %get-tuple-element.12) | copy-start | bytes 393220
  103.1 2.1 %copy-start.11 = (f32[1,1,256,1,128]{2,1,4,3,0:T(1,128)S(1)}, f32[1,1,256,1,128]{2,1,4,3,0:T(1,128)}, u32[]{:S(2)}) copy-start(f32[1,1,256,1,128]{2,1,4,3,0:T(1,128)} %get-tuple-element.13) | copy-start | bytes 393220
  103.6 2.2 %copy-start.8 = (f32[256,128]{0,1:T(8,128)S(1)}, f32[256,128]{0,1:T(8,128)}, u32[]{:S(2)}) copy-start(f32[256,128]{0,1:T(8,128)} %copy.108) | copy-start | bytes 393220
  113.6 29.0 %copy-start.1 = (bf16[256,2,1024]{2,1,0:T(2,128)(2,1)S(1)}, bf16[256,2,1024]{2,1,0:T(2,128)(2,1)}, u32[]{:S(2)}) copy-start(bf16[256,2,1024]{2,1,0:T(2,128)(2,1)} %param.18) | copy-start | bytes 3145732
Sparse Core Ops, SparseCore 0:
  119.5 21.4 reduce-scatter.1

commit v2 on v1

--- a/solution.py
+++ b/solution.py
@@ -1,7 +1,11 @@
+import functools
+
 import jax
 import jax.numpy as jnp
 import numpy as np
 from jax import lax
+from jax.experimental import pallas as pl
+from jax.experimental.pallas import tpu as pltpu
 from jax.sharding import PartitionSpec as P
 
 
@@ -23,7 +27,7 @@
     return jnp.dot(a, b, preferred_element_type=jnp.float32)
 
 
-def per_device(inputs, gain, w_in, w_out, history, filt_far, filt_near):
+def plain_layer(inputs, gain, w_in, w_out, history, filt_far, filt_near):
     chan_width = inputs.shape[1]
     block = filt_near.shape[0]
     ctx_index = lax.axis_index("ctx")
@@ -112,6 +116,308 @@
     return (mixed, gated)
 
 
+MESH = pl.DeviceIdType.MESH
+
+
+def layer_kernel(
+    n, cn, inputs, gain, w_in, w_out, history, filt_far, filt_near, fwd_hi, fwd_lo, inv_hi, inv_lo,
+    mixed, gated,
+    x_all, normed, win, wout, h_stage, f_stage, h_all, f_all, near, wide, h_spec, f_spec, total,
+    acc, fresh_out, fresh_all, back_out, g_all, m_all, m_full, part, part_all,
+    x_local, x_send, x_recv, hs_sem, fs_sem, win_sem, wout_sem, near_sem,
+    h_send, h_recv, f_send, f_recv, v_send, v_recv, g_send, g_recv, m_send, m_recv, p_send, p_recv,
+):
+    me = lax.axis_index("ctx")
+    mine = lax.axis_index("chan")
+    rows, width = inputs.shape
+    block = history.shape[0]
+    cols = width // n
+
+    def lanes(d):
+        return pl.ds(pl.multiple_of(d * cols, 128), cols)
+
+    def remote(src, dst, send, recv, where):
+        return pltpu.make_async_remote_copy(
+            src_ref=src, dst_ref=dst, send_sem=send, recv_sem=recv,
+            device_id=where, device_id_type=MESH,
+        )
+
+    def ctx_peer(s):
+        return lax.rem(me + s, n)
+
+    def chan_peer(s):
+        return lax.rem(mine + s, cn)
+
+    x_copy = pltpu.make_async_copy(inputs, x_all.at[mine], x_local)
+    x_copy.start()
+    h_local, f_local = [], []
+    for s in range(n):
+        d = ctx_peer(s)
+        h_to = h_all.at[me] if s == 0 else h_stage.at[s - 1]
+        f_to = f_all.at[me] if s == 0 else f_stage.at[s - 1]
+        h_local.append(pltpu.make_async_copy(history.at[:, :, lanes(d)], h_to, hs_sem.at[s]))
+        f_local.append(pltpu.make_async_copy(filt_far.at[:, :, lanes(d)], f_to, fs_sem.at[s]))
+    near_copy = pltpu.make_async_copy(filt_near.at[:, :, lanes(me)], near, near_sem)
+    order = list(range(2, n)) + [1, 0]
+    for s in order:
+        h_local[s].start()
+        f_local[s].start()
+    near_copy.start()
+    win_copies = []
+    for i in range(3):
+        for j in range(cn):
+            copy = pltpu.make_async_copy(
+                w_in.at[i, pl.ds(j * width, width)], win.at[i * cn + j], win_sem.at[i * cn + j]
+            )
+            copy.start()
+            win_copies.append(copy)
+    wout_copies = []
+    for j in range(cn):
+        copy = pltpu.make_async_copy(
+            w_out.at[:, pl.ds(j * width, width)], wout.at[j], wout_sem.at[j]
+        )
+        copy.start()
+        wout_copies.append(copy)
+
+    barrier = pltpu.get_barrier_semaphore()
+    for s in range(1, n):
+        pl.semaphore_signal(barrier, inc=1, device_id={"ctx": ctx_peer(s)}, device_id_type=MESH)
+    for s in range(1, cn):
+        pl.semaphore_signal(barrier, inc=1, device_id={"chan": chan_peer(s)}, device_id_type=MESH)
+    pl.semaphore_wait(barrier, n + cn - 2)
+
+    x_copies = []
+    for s in range(1, cn):
+        copy = remote(
+            inputs, x_all.at[mine], x_send.at[s], x_recv.at[s], {"chan": chan_peer(s)}
+        )
+        copy.start()
+        x_copies.append(copy)
+    h_copies, f_copies = [None] * n, [None] * n
+    for s in order[:-1]:
+        where = {"ctx": ctx_peer(s)}
+        h_local[s].wait()
+        h_copies[s] = remote(h_stage.at[s - 1], h_all.at[me], h_send.at[s], h_recv.at[s], where)
+        h_copies[s].start()
+        f_local[s].wait()
+        f_copies[s] = remote(f_stage.at[s - 1], f_all.at[me], f_send.at[s], f_recv.at[s], where)
+        f_copies[s].start()
+
+    def forward(x):
+        return times(fwd_hi[...], x) + times(fwd_lo[...], x)
+
+    def halves(ref):
+        wide[...] = ref.reshape(2 * block, cols)[...].astype(jnp.float32)
+        return [
+            wide[pl.ds(c, block, stride=2), :].astype(jnp.bfloat16) for c in range(2)
+        ]
+
+    def transform(k):
+        x = jnp.concatenate(halves(h_all.at[k]) + halves(f_all.at[k]), axis=1)
+        spec = forward(x)
+        h_spec[k] = spec[:, : 2 * cols]
+        f_spec[k] = spec[:, 2 * cols :]
+
+    h_local[0].wait()
+    f_local[0].wait()
+    near_copy.wait()
+    f_spec[n] = forward(jnp.concatenate(halves(near), axis=1))
+    transform(me)
+
+    x_copy.wait()
+    for copy in x_copies:
+        copy.wait_recv()
+    square = jnp.zeros((rows, 1), jnp.float32)
+    for j in range(cn):
+        part_x = x_all[j].astype(jnp.float32)
+        square = square + jnp.sum(part_x * part_x, axis=-1, keepdims=True)
+    scale = lax.rsqrt(square / (cn * width) + 1e-06)
+    for j in range(cn):
+        normed[j] = (x_all[j].astype(jnp.float32) * scale * gain[j : j + 1, :]).astype(jnp.bfloat16)
+
+    for i in range(3):
+        for j in range(cn):
+            win_copies[i * cn + j].wait()
+
+        @pl.loop(0, n // 2 if n % 2 == 0 else n)
+        def _(q):
+            step = 2 if n % 2 == 0 else 1
+            span = step * cols
+            at = pl.ds(pl.multiple_of(q * span, 128), span)
+            proj = times(normed[0], win[i * cn, :, at])
+            for j in range(1, cn):
+                proj = proj + times(normed[j], win[i * cn + j, :, at])
+            for p in range(step):
+                fresh_out[q * step + p, i] = proj[:, p * cols : (p + 1) * cols].astype(jnp.bfloat16)
+
+    v_local = pltpu.make_async_copy(fresh_out.at[me], fresh_all.at[me], v_recv.at[0])
+    v_local.start()
+    v_copies = []
+    for s in range(1, n):
+        d = ctx_peer(s)
+        copy = remote(
+            fresh_out.at[d], fresh_all.at[me], v_send.at[s], v_recv.at[s], {"ctx": d}
+        )
+        copy.start()
+        v_copies.append(copy)
+
+    for s in [1] + list(range(2, n)):
+        h_copies[s].wait_recv()
+        f_copies[s].wait_recv()
+        transform(lax.rem(me + n - s, n))
+
+    chunk = 32
+
+    @pl.loop(0, block // chunk)
+    def _(r):
+        low = pl.ds(pl.multiple_of(r * chunk, chunk), chunk)
+        high = pl.ds(pl.multiple_of(block + r * chunk, chunk), chunk)
+        odd = lax.broadcasted_iota(jnp.int32, (chunk, 2 * cols), 0) % 2
+        turn = 1.0 - 2.0 * odd.astype(jnp.float32)
+        sum_re = jnp.zeros((chunk, 2 * cols), jnp.float32)
+        sum_im = jnp.zeros((chunk, 2 * cols), jnp.float32)
+        for k in range(n):
+            win_re = f_spec[k, low, :] + turn * f_spec[k + 1, high, :]
+            win_im = f_spec[k, high, :] - turn * f_spec[k + 1, low, :]
+            old_re, old_im = h_spec[k, low, :], h_spec[k, high, :]
+            sum_re = sum_re + win_re * old_re + win_im * old_im
+            sum_im = sum_im + win_im * old_re - win_re * old_im
+        acc[low, :] = sum_re
+        acc[high, :] = sum_im
+
+    def whole_conv(which, values):
+        at = slice(which * cols, (which + 1) * cols)
+        new = forward(values)
+        new_re, new_im = new[:block], new[block:]
+        near_re, near_im = f_spec[n, :block, at], f_spec[n, block:, at]
+        all_re = acc[:block, at] + near_re * new_re + near_im * new_im
+        all_im = acc[block:, at] + near_im * new_re - near_re * new_im
+        whole = jnp.concatenate([all_re, all_im], axis=0)
+        high = whole.astype(jnp.bfloat16)
+        low = (whole - high.astype(jnp.float32)).astype(jnp.bfloat16)
+        both = times(inv_hi[...], jnp.concatenate([high, low], axis=1))
+        return both[:, :cols] + both[:, cols:] + times(inv_lo[...], high)
+
+    def send_back(index, every, send, recv):
+        local = pltpu.make_async_copy(back_out.at[index, me], every.at[me], recv.at[0])
+        local.start()
+        copies = []
+        for s in range(1, n):
+            d = ctx_peer(s)
+            copy = remote(
+                back_out.at[index, d], every.at[me], send.at[s], recv.at[s], {"ctx": d}
+            )
+            copy.start()
+            copies.append(copy)
+        return local, copies
+
+    v_local.wait()
+    for copy in v_copies:
+        copy.wait_recv()
+    fresh_rows = n * rows
+    first = whole_conv(0, fresh_all[:, 0].reshape(fresh_rows, cols))
+    gate_one = fresh_all[:, 1].reshape(fresh_rows, cols).astype(jnp.float32)
+    gated_cols = (gate_one * first).astype(jnp.bfloat16)
+    back_out[0] = gated_cols.reshape(n, rows, cols)
+    g_local, g_copies = send_back(0, g_all, g_send, g_recv)
+    second = whole_conv(1, gated_cols)
+    gate_two = fresh_all[:, 2].reshape(fresh_rows, cols).astype(jnp.float32)
+    back_out[1] = (gate_two * second).astype(jnp.bfloat16).reshape(n, rows, cols)
+    m_local, m_copies = send_back(1, m_all, m_send, m_recv)
+
+    g_local.wait()
+    for copy in g_copies:
+        copy.wait_recv()
+    for j in range(n):
+        gated[:, j * cols : (j + 1) * cols] = g_all[j]
+    for copy in wout_copies:
+        copy.wait()
+    m_local.wait()
+    for copy in m_copies:
+        copy.wait_recv()
+    for j in range(n):
+        m_full[:, j * cols : (j + 1) * cols] = m_all[j]
+    p_copies = []
+    for s in list(range(1, cn)) + [0]:
+        d = chan_peer(s)
+        part[s] = times(m_full[...], wout[d])
+        if s > 0:
+            copy = remote(part.at[s], part_all.at[s], p_send.at[s], p_recv.at[s], {"chan": d})
+            copy.start()
+            p_copies.append(copy)
+    result = part[0]
+    for s, copy in enumerate(p_copies):
+        copy.wait_recv()
+        result = result + part_all[s + 1]
+    mixed[...] = result.astype(jnp.bfloat16)
+
+    for copy in x_copies + h_copies[1:] + f_copies[1:] + v_copies + g_copies + m_copies + p_copies:
+        copy.wait_send()
+
+
+def fused_layer(inputs, gain, w_in, w_out, history, filt_far, filt_near):
+    n, cn = lax.axis_size("ctx"), lax.axis_size("chan")
+    rows, width = inputs.shape
+    block = history.shape[0]
+    cols = width // n
+    (fwd_hi, fwd_lo), (inv_hi, inv_lo), _ = transforms(block)
+    f32, bf16 = jnp.float32, jnp.bfloat16
+    vmem = pl.BlockSpec(memory_space=pltpu.VMEM)
+    anywhere = pl.BlockSpec(memory_space=pl.ANY)
+    dma = pltpu.SemaphoreType.DMA
+    return pl.pallas_call(
+        functools.partial(layer_kernel, n, cn),
+        out_shape=(jax.ShapeDtypeStruct((rows, width), bf16),) * 2,
+        in_specs=[anywhere, vmem] + [anywhere] * 5 + [vmem] * 4,
+        out_specs=(vmem, vmem),
+        scratch_shapes=[
+            pltpu.VMEM((cn, rows, width), bf16),
+            pltpu.VMEM((cn, rows, width), bf16),
+            pltpu.VMEM((3 * cn, width, width), bf16),
+            pltpu.VMEM((cn, width, width), bf16),
+            pltpu.VMEM((n - 1, block, 2, cols), bf16),
+            pltpu.VMEM((n - 1, block, 2, cols), bf16),
+            pltpu.VMEM((n, block, 2, cols), bf16),
+            pltpu.VMEM((n, block, 2, cols), bf16),
+            pltpu.VMEM((block, 2, cols), bf16),
+            pltpu.VMEM((2 * block, cols), f32),
+            pltpu.VMEM((n, 2 * block, 2 * cols), f32),
+            pltpu.VMEM((n + 1, 2 * block, 2 * cols), f32),
+            pltpu.VMEM((8, 128), f32),
+            pltpu.VMEM((2 * block, 2 * cols), f32),
+            pltpu.VMEM((n, 3, rows, cols), bf16),
+            pltpu.VMEM((n, 3, rows, cols), bf16),
+            pltpu.VMEM((2, n, rows, cols), bf16),
+            pltpu.VMEM((n, rows, cols), bf16),
+            pltpu.VMEM((n, rows, cols), bf16),
+            pltpu.VMEM((rows, width), bf16),
+            pltpu.VMEM((cn, rows, width), f32),
+            pltpu.VMEM((cn, rows, width), f32),
+            dma, dma((cn,)), dma((cn,)), dma((n,)), dma((n,)), dma((3 * cn,)), dma((cn,)), dma,
+        ]
+        + [dma((n,))] * 10
+        + [dma((cn,))] * 2,
+        compiler_params=pltpu.CompilerParams(
+            collective_id=0, has_side_effects=True, vmem_limit_bytes=60 * 1024 * 1024
+        ),
+    )(
+        inputs, gain.reshape(cn, width), w_in.transpose(1, 0, 2), w_out, history, filt_far,
+        filt_near, fwd_hi, fwd_lo, inv_hi, inv_lo,
+    )
+
+
+def per_device(inputs, gain, w_in, w_out, history, filt_far, filt_near):
+    n = lax.axis_size("ctx")
+    rows, width = inputs.shape
+    fits = (
+        width % (128 * n) == 0
+        and rows % 16 == 0
+        and history.shape[0] == filt_near.shape[0] == n * rows
+    )
+    layer = fused_layer if fits else plain_layer
+    return layer(inputs, gain, w_in, w_out, history, filt_far, filt_near)
+
+
 def solution(mesh):
     placed = (
         P("ctx", "chan"),

time: 150 us -> 61.1 us (0.41)
  Pallas kernels: 0 us -> 55.9 us
  blocking collectives: 30.8 us -> 0 us
  matrix products: 29.2 us -> 0 us
  waiting for transfers between devices: 27.4 us -> 0 us
  starting transfers between devices: 20.1 us -> 0 us
  local copies, waits for them, and re-layouts: 22.4 us -> 4.28 us
  between operations: 14.5 us -> 0.64 us
  other arithmetic: 5.08 us -> 0 us
    pallas_call x0 -> x1, Pallas kernels: none -> 55.9 us  [fused_layer(): pl.pallas_call(functools.partial(layer_kernel, n, cn), out_shape=(jax.Sha...]
    dot_general x20 -> x0, matrix products: 29.2 us -> none  [the longest x19 23.4 us: times(): return jnp.dot(a, b, preferred_element_type=jnp.float32)]
    all_to_all x5 -> x0, starting transfers between devices: 19.8 us -> none  [the longest x3 12.1 us: per_device(): lax.all_to_all(times(normed, weights[i]).astype(jnp.bfloat16), 'ctx', spl...]
    all_gather x1 -> x0, blocking collectives: 16 us -> none  [per_device(): gathered = lax.all_gather(inputs, 'chan', axis=1, tiled=True)]
    all_to_all x2 -> x0, blocking collectives: 14.8 us -> none  [the longest x1 7.4 us: per_device(): lax.all_to_all(mixed_cols, 'ctx', split_axis=0, concat_axis=1, tiled=True)]
    all_to_all x5 -> x0, waiting for transfers between devices: 13.9 us -> none  [the longest x1 8.69 us: per_device(): lax.all_to_all(history, 'ctx', split_axis=2, concat_axis=0, tiled=True)]
    reduce_scatter x1 -> x0, waiting for transfers between devices: 13.5 us -> none  [per_device(): lax.psum_scatter(partial_out, 'chan', scatter_dimension=1, tiled=True)]
    unnamed x40 -> x2, local copies, waits for them, and re-layouts: 15.3 us -> 2.95 us
  transfers between devices with their start and end apart: 6 -> 0, of which waited for: 3 -> 0; matrix products, arithmetic and copies ran while one was open for 22% -> 0% of each run, Pallas kernels for 0% -> 0%
where the time goes in v2:
time: 61.1 us; the launch traced here: 60.8 us
  Pallas kernels  55.9 us (91%)
  local copies, waits for them, and re-layouts  4.28 us (7%)
  between operations  0.64 us (1%)
    pallas_call x1, Pallas kernels, fused_layer(): pl.pallas_call(functools.partial(layer_kernel, n, cn), out_shape=(jax.Sha...  55.9 us
    unnamed x2, local copies, waits for them, and re-layouts  2.95 us
    reshape x1, local copies, waits for them, and re-layouts, fused_layer(): gain.reshape(cn, width)  1.33 us

profile of v2, /device:TPU:0, one launch (start us, length us, event | category | flops | bytes accessed | tf_op | source)
XLA Modules:
  0.0 60.8 jit_solution(15657010955007254824)
XLA Ops:
  0.6 1.3 %reshape.7.gain = f32[4,1024]{1,0:T(4,128)} reshape(f32[4096]{0:T(1024)} %param.12) | data formatting | bytes 32768 | tf_op jit(solution)/shard_map/reshape | solution.py:404
  2.0 55.9 %shard_map.122 = (bf16[32,1024]{1,0:T(8,128)(2,1)}, bf16[32,1024]{1,0:T(8,128)(2,1)}) custom-call(bf16[32,1024]{1,0:T(8,128)(2,1)} %inputs.1, f32[4,1024]{1,0:T(4,128)} %reshape.7.gain, bf16[3,4096,1024]{2,1,0:T(8,128)(2,1)} %bitcast.1, bf16[1024,4096]{1,0:T(8,128)(2,1)} %w_out.1, bf16[256,2,1024]{2,1,0:T(2,128)(2,1)} %history.1, ...), custom_call_target="tpu_custom_call" | custom-call | tf_op jit(solution)/shard_map/pallas_call | solution.py:368
  57.9 1.5 %copy.15 = bf16[32,1024]{1,0:T(8,128)(2,1)} copy(bf16[32,1024]{1,0:T(8,128)(2,1)} %get-tuple-element.4) | data formatting | bytes 131072
  59.4 1.5 %copy.16 = bf16[32,1024]{1,0:T(8,128)(2,1)} copy(bf16[32,1024]{1,0:T(8,128)(2,1)} %get-tuple-element.5) | data formatting | bytes 131072

commit v3 on v2

--- a/solution.py
+++ b/solution.py
@@ -121,8 +121,8 @@
 
 def layer_kernel(
     n, cn, inputs, gain, w_in, w_out, history, filt_far, filt_near, fwd_hi, fwd_lo, inv_hi, inv_lo,
-    mixed, gated,
-    x_all, normed, win, wout, h_stage, f_stage, h_all, f_all, near, wide, h_spec, f_spec, total,
+    out,
+    x_all, normed, win, wout, h_stage, f_stage, h_all, f_all, near, wide, h_spec, f_spec,
     acc, fresh_out, fresh_all, back_out, g_all, m_all, m_full, part, part_all,
     x_local, x_send, x_recv, hs_sem, fs_sem, win_sem, wout_sem, near_sem,
     h_send, h_recv, f_send, f_recv, v_send, v_recv, g_send, g_recv, m_send, m_recv, p_send, p_recv,
@@ -158,7 +158,7 @@
         h_local.append(pltpu.make_async_copy(history.at[:, :, lanes(d)], h_to, hs_sem.at[s]))
         f_local.append(pltpu.make_async_copy(filt_far.at[:, :, lanes(d)], f_to, fs_sem.at[s]))
     near_copy = pltpu.make_async_copy(filt_near.at[:, :, lanes(me)], near, near_sem)
-    order = list(range(2, n)) + [1, 0]
+    order = list(range(1, n)) + [0]
     for s in order:
         h_local[s].start()
         f_local[s].start()
@@ -233,7 +233,7 @@
         square = square + jnp.sum(part_x * part_x, axis=-1, keepdims=True)
     scale = lax.rsqrt(square / (cn * width) + 1e-06)
     for j in range(cn):
-        normed[j] = (x_all[j].astype(jnp.float32) * scale * gain[j : j + 1, :]).astype(jnp.bfloat16)
+        normed[j] = (x_all[j].astype(jnp.float32) * scale * gain[:, j * width : (j + 1) * width]).astype(jnp.bfloat16)
 
     for i in range(3):
         for j in range(cn):
@@ -261,38 +261,50 @@
         copy.start()
         v_copies.append(copy)
 
-    for s in [1] + list(range(2, n)):
-        h_copies[s].wait_recv()
-        f_copies[s].wait_recv()
-        transform(lax.rem(me + n - s, n))
-
     chunk = 32
 
-    @pl.loop(0, block // chunk)
-    def _(r):
-        low = pl.ds(pl.multiple_of(r * chunk, chunk), chunk)
-        high = pl.ds(pl.multiple_of(block + r * chunk, chunk), chunk)
-        odd = lax.broadcasted_iota(jnp.int32, (chunk, 2 * cols), 0) % 2
-        turn = 1.0 - 2.0 * odd.astype(jnp.float32)
-        sum_re = jnp.zeros((chunk, 2 * cols), jnp.float32)
-        sum_im = jnp.zeros((chunk, 2 * cols), jnp.float32)
-        for k in range(n):
+    def add_term(k, first):
+        @pl.loop(0, block // chunk)
+        def _(r):
+            low = pl.ds(pl.multiple_of(r * chunk, chunk), chunk)
+            high = pl.ds(pl.multiple_of(block + r * chunk, chunk), chunk)
+            odd = lax.broadcasted_iota(jnp.int32, (chunk, 2 * cols), 0) % 2
+            turn = 1.0 - 2.0 * odd.astype(jnp.float32)
             win_re = f_spec[k, low, :] + turn * f_spec[k + 1, high, :]
             win_im = f_spec[k, high, :] - turn * f_spec[k + 1, low, :]
             old_re, old_im = h_spec[k, low, :], h_spec[k, high, :]
-            sum_re = sum_re + win_re * old_re + win_im * old_im
-            sum_im = sum_im + win_im * old_re - win_re * old_im
-        acc[low, :] = sum_re
-        acc[high, :] = sum_im
-
-    def whole_conv(which, values):
+            sum_re = win_re * old_re + win_im * old_im
+            sum_im = win_im * old_re - win_re * old_im
+            if not first:
+                sum_re = sum_re + acc[low, :]
+                sum_im = sum_im + acc[high, :]
+            acc[low, :] = sum_re
+            acc[high, :] = sum_im
+
+    def add_fresh(which, values):
         at = slice(which * cols, (which + 1) * cols)
         new = forward(values)
         new_re, new_im = new[:block], new[block:]
         near_re, near_im = f_spec[n, :block, at], f_spec[n, block:, at]
-        all_re = acc[:block, at] + near_re * new_re + near_im * new_im
-        all_im = acc[block:, at] + near_im * new_re - near_re * new_im
-        whole = jnp.concatenate([all_re, all_im], axis=0)
+        acc[:block, at] += near_re * new_re + near_im * new_im
+        acc[block:, at] += near_im * new_re - near_re * new_im
+
+    fresh_rows = n * rows
+    for s in range(1, n):
+        if s == n - 1:
+            v_local.wait()
+            for copy in v_copies:
+                copy.wait_recv()
+            add_fresh(0, fresh_all[:, 0].reshape(fresh_rows, cols))
+        h_copies[s].wait_recv()
+        f_copies[s].wait_recv()
+        k = lax.rem(me + n - s, n)
+        transform(k)
+        add_term(k, s == 1)
+    add_term(me, False)
+
+    def inverse(which):
+        whole = acc[:, which * cols : (which + 1) * cols]
         high = whole.astype(jnp.bfloat16)
         low = (whole - high.astype(jnp.float32)).astype(jnp.bfloat16)
         both = times(inv_hi[...], jnp.concatenate([high, low], axis=1))
@@ -311,16 +323,13 @@
             copies.append(copy)
         return local, copies
 
-    v_local.wait()
-    for copy in v_copies:
-        copy.wait_recv()
-    fresh_rows = n * rows
-    first = whole_conv(0, fresh_all[:, 0].reshape(fresh_rows, cols))
+    first = inverse(0)
     gate_one = fresh_all[:, 1].reshape(fresh_rows, cols).astype(jnp.float32)
     gated_cols = (gate_one * first).astype(jnp.bfloat16)
     back_out[0] = gated_cols.reshape(n, rows, cols)
     g_local, g_copies = send_back(0, g_all, g_send, g_recv)
-    second = whole_conv(1, gated_cols)
+    add_fresh(1, gated_cols)
+    second = inverse(1)
     gate_two = fresh_all[:, 2].reshape(fresh_rows, cols).astype(jnp.float32)
     back_out[1] = (gate_two * second).astype(jnp.bfloat16).reshape(n, rows, cols)
     m_local, m_copies = send_back(1, m_all, m_send, m_recv)
@@ -329,7 +338,7 @@
     for copy in g_copies:
         copy.wait_recv()
     for j in range(n):
-        gated[:, j * cols : (j + 1) * cols] = g_all[j]
+        out[1, :, j * cols : (j + 1) * cols] = g_all[j]
     for copy in wout_copies:
         copy.wait()
     m_local.wait()
@@ -340,16 +349,17 @@
     p_copies = []
     for s in list(range(1, cn)) + [0]:
         d = chan_peer(s)
-        part[s] = times(m_full[...], wout[d])
+        product = times(m_full[...], wout[d])
         if s > 0:
+            part[s] = product.astype(jnp.bfloat16)
             copy = remote(part.at[s], part_all.at[s], p_send.at[s], p_recv.at[s], {"chan": d})
             copy.start()
             p_copies.append(copy)
-    result = part[0]
+    result = product
     for s, copy in enumerate(p_copies):
         copy.wait_recv()
-        result = result + part_all[s + 1]
-    mixed[...] = result.astype(jnp.bfloat16)
+        result = result + part_all[s + 1].astype(jnp.float32)
+    out[0] = result.astype(jnp.bfloat16)
 
     for copy in x_copies + h_copies[1:] + f_copies[1:] + v_copies + g_copies + m_copies + p_copies:
         copy.wait_send()
@@ -365,11 +375,11 @@
     vmem = pl.BlockSpec(memory_space=pltpu.VMEM)
     anywhere = pl.BlockSpec(memory_space=pl.ANY)
     dma = pltpu.SemaphoreType.DMA
-    return pl.pallas_call(
+    both = pl.pallas_call(
         functools.partial(layer_kernel, n, cn),
-        out_shape=(jax.ShapeDtypeStruct((rows, width), bf16),) * 2,
+        out_shape=jax.ShapeDtypeStruct((2, rows, width), bf16),
         in_specs=[anywhere, vmem] + [anywhere] * 5 + [vmem] * 4,
-        out_specs=(vmem, vmem),
+        out_specs=vmem,
         scratch_shapes=[
             pltpu.VMEM((cn, rows, width), bf16),
             pltpu.VMEM((cn, rows, width), bf16),
@@ -383,7 +393,6 @@
             pltpu.VMEM((2 * block, cols), f32),
             pltpu.VMEM((n, 2 * block, 2 * cols), f32),
             pltpu.VMEM((n + 1, 2 * block, 2 * cols), f32),
-            pltpu.VMEM((8, 128), f32),
             pltpu.VMEM((2 * block, 2 * cols), f32),
             pltpu.VMEM((n, 3, rows, cols), bf16),
             pltpu.VMEM((n, 3, rows, cols), bf16),
@@ -391,8 +400,8 @@
             pltpu.VMEM((n, rows, cols), bf16),
             pltpu.VMEM((n, rows, cols), bf16),
             pltpu.VMEM((rows, width), bf16),
-            pltpu.VMEM((cn, rows, width), f32),
-            pltpu.VMEM((cn, rows, width), f32),
+            pltpu.VMEM((cn, rows, width), bf16),
+            pltpu.VMEM((cn, rows, width), bf16),
             dma, dma((cn,)), dma((cn,)), dma((n,)), dma((n,)), dma((3 * cn,)), dma((cn,)), dma,
         ]
         + [dma((n,))] * 10
@@ -401,9 +410,10 @@
             collective_id=0, has_side_effects=True, vmem_limit_bytes=60 * 1024 * 1024
         ),
     )(
-        inputs, gain.reshape(cn, width), w_in.transpose(1, 0, 2), w_out, history, filt_far,
+        inputs, gain.reshape(1, cn * width), w_in.transpose(1, 0, 2), w_out, history, filt_far,
         filt_near, fwd_hi, fwd_lo, inv_hi, inv_lo,
     )
+    return both[0], both[1]
 
 
 def per_device(inputs, gain, w_in, w_out, history, filt_far, filt_near):

time: 61.1 us -> 54.1 us (0.89)
  Pallas kernels: 55.9 us -> 51.8 us
  local copies, waits for them, and re-layouts: 4.28 us -> 1.53 us
    pallas_call x1, Pallas kernels: 55.9 us -> 51.8 us  [fused_layer(): pl.pallas_call(functools.partial(layer_kernel, n, cn), out_shape=jax.Shap...]
    unnamed x2 -> x0, local copies, waits for them, and re-layouts: 2.95 us -> none
    squeeze x0 -> x1, local copies, waits for them, and re-layouts: none -> 1.53 us  [fused_layer(): return (both[0], both[1])]
    reshape x1 -> x0, local copies, waits for them, and re-layouts: 1.33 us -> none  [fused_layer(): gain.reshape(cn, width)]
where the time goes in v3:
time: 54.1 us; the launch traced here: 54 us
  Pallas kernels  51.8 us (96%)
  local copies, waits for them, and re-layouts  1.53 us (3%)
  between operations  0.64 us (1%)
    pallas_call x1, Pallas kernels, fused_layer(): pl.pallas_call(functools.partial(layer_kernel, n, cn), out_shape=jax.Shap...  51.8 us
    squeeze x1, local copies, waits for them, and re-layouts, fused_layer(): return (both[0], both[1])  1.53 us

profile of v3, /device:TPU:0, one launch (start us, length us, event | category | flops | bytes accessed | tf_op | source)
XLA Modules:
  0.0 54.0 jit_solution(1586644851558828104)
XLA Ops:
  0.6 51.8 %shard_map.122 = bf16[2,32,1024]{2,1,0:T(8,128)(2,1)} custom-call(bf16[32,1024]{1,0:T(8,128)(2,1)} %inputs.1, f32[1,4096]{1,0:T(1,128)} %bitcast.7, bf16[3,4096,1024]{2,1,0:T(8,128)(2,1)} %bitcast.6, bf16[1024,4096]{1,0:T(8,128)(2,1)} %w_out.1, bf16[256,2,1024]{2,1,0:T(2,128)(2,1)} %history.1, bf16[256,2,1024]{2,1,0:T(2,128)(2,1)} %filt_far.1, ...), custom_call_target="tpu_custom_call" | custom-call | tf_op jit(solution)/shard_map/pallas_call | solution.py:378
  52.4 1.5 %slice_bitcast_fusion = (bf16[32,1024]{1,0:T(8,128)(2,1)}, bf16[32,1024]{1,0:T(8,128)(2,1)}) fusion(bf16[2,32,1024]{2,1,0:T(8,128)(2,1)} %shard_map.122), kind=kLoop, calls=%fused_computation | loop fusion | bytes 262144 | tf_op jit(solution)/shard_map/squeeze | solution.py:416

commit v4 on v3

--- a/solution.py
+++ b/solution.py
@@ -120,8 +120,8 @@
 
 
 def layer_kernel(
-    n, cn, inputs, gain, w_in, w_out, history, filt_far, filt_near, fwd_hi, fwd_lo, inv_hi, inv_lo,
-    out,
+    n, cn, inputs, gain_hbm, w_in, w_out, history, filt_far, filt_near,
+    fwd_hi_hbm, fwd_lo_hbm, inv_hi_hbm, inv_lo_hbm, out, gain, fwd_hi, fwd_lo, inv_hi, inv_lo, table_sem,
     x_all, normed, win, wout, h_stage, f_stage, h_all, f_all, near, wide, h_spec, f_spec,
     acc, fresh_out, fresh_all, back_out, g_all, m_all, m_full, part, part_all,
     x_local, x_send, x_recv, hs_sem, fs_sem, win_sem, wout_sem, near_sem,
@@ -147,6 +147,12 @@
 
     def chan_peer(s):
         return lax.rem(mine + s, cn)
+
+    barrier = pltpu.get_barrier_semaphore()
+    for s in range(1, n):
+        pl.semaphore_signal(barrier, inc=1, device_id={"ctx": ctx_peer(s)}, device_id_type=MESH)
+    for s in range(1, cn):
+        pl.semaphore_signal(barrier, inc=1, device_id={"chan": chan_peer(s)}, device_id_type=MESH)
 
     x_copy = pltpu.make_async_copy(inputs, x_all.at[mine], x_local)
     x_copy.start()
@@ -163,6 +169,35 @@
         h_local[s].start()
         f_local[s].start()
     near_copy.start()
+    table_copies = []
+    for at, (source, table) in enumerate(
+        [
+            (fwd_hi_hbm, fwd_hi), (fwd_lo_hbm, fwd_lo), (gain_hbm, gain),
+            (inv_hi_hbm, inv_hi), (inv_lo_hbm, inv_lo),
+        ]
+    ):
+        copy = pltpu.make_async_copy(source, table, table_sem.at[at])
+        copy.start()
+        table_copies.append(copy)
+    pl.semaphore_wait(barrier, n + cn - 2)
+
+    x_copies = []
+    for s in range(1, cn):
+        copy = remote(
+            inputs, x_all.at[mine], x_send.at[s], x_recv.at[s], {"chan": chan_peer(s)}
+        )
+        copy.start()
+        x_copies.append(copy)
+    h_copies, f_copies = [None] * n, [None] * n
+    for s in order[:-1]:
+        where = {"ctx": ctx_peer(s)}
+        h_local[s].wait()
+        h_copies[s] = remote(h_stage.at[s - 1], h_all.at[me], h_send.at[s], h_recv.at[s], where)
+        h_copies[s].start()
+        f_local[s].wait()
+        f_copies[s] = remote(f_stage.at[s - 1], f_all.at[me], f_send.at[s], f_recv.at[s], where)
+        f_copies[s].start()
+
     win_copies = []
     for i in range(3):
         for j in range(cn):
@@ -179,30 +214,6 @@
         copy.start()
         wout_copies.append(copy)
 
-    barrier = pltpu.get_barrier_semaphore()
-    for s in range(1, n):
-        pl.semaphore_signal(barrier, inc=1, device_id={"ctx": ctx_peer(s)}, device_id_type=MESH)
-    for s in range(1, cn):
-        pl.semaphore_signal(barrier, inc=1, device_id={"chan": chan_peer(s)}, device_id_type=MESH)
-    pl.semaphore_wait(barrier, n + cn - 2)
-
-    x_copies = []
-    for s in range(1, cn):
-        copy = remote(
-            inputs, x_all.at[mine], x_send.at[s], x_recv.at[s], {"chan": chan_peer(s)}
-        )
-        copy.start()
-        x_copies.append(copy)
-    h_copies, f_copies = [None] * n, [None] * n
-    for s in order[:-1]:
-        where = {"ctx": ctx_peer(s)}
-        h_local[s].wait()
-        h_copies[s] = remote(h_stage.at[s - 1], h_all.at[me], h_send.at[s], h_recv.at[s], where)
-        h_copies[s].start()
-        f_local[s].wait()
-        f_copies[s] = remote(f_stage.at[s - 1], f_all.at[me], f_send.at[s], f_recv.at[s], where)
-        f_copies[s].start()
-
     def forward(x):
         return times(fwd_hi[...], x) + times(fwd_lo[...], x)
 
@@ -221,6 +232,8 @@
     h_local[0].wait()
     f_local[0].wait()
     near_copy.wait()
+    for copy in table_copies:
+        copy.wait()
     f_spec[n] = forward(jnp.concatenate(halves(near), axis=1))
     transform(me)
 
@@ -347,21 +360,22 @@
     for j in range(n):
         m_full[:, j * cols : (j + 1) * cols] = m_all[j]
     p_copies = []
-    for s in list(range(1, cn)) + [0]:
+    half = cn // 2
+    for s in [half] + [s for s in range(1, cn) if s != half] + [0]:
         d = chan_peer(s)
         product = times(m_full[...], wout[d])
         if s > 0:
             part[s] = product.astype(jnp.bfloat16)
             copy = remote(part.at[s], part_all.at[s], p_send.at[s], p_recv.at[s], {"chan": d})
             copy.start()
-            p_copies.append(copy)
+            p_copies.append((s, copy))
     result = product
-    for s, copy in enumerate(p_copies):
+    for s, copy in p_copies:
         copy.wait_recv()
-        result = result + part_all[s + 1].astype(jnp.float32)
+        result = result + part_all[s].astype(jnp.float32)
     out[0] = result.astype(jnp.bfloat16)
 
-    for copy in x_copies + h_copies[1:] + f_copies[1:] + v_copies + g_copies + m_copies + p_copies:
+    for copy in x_copies + h_copies[1:] + f_copies[1:] + v_copies + g_copies + m_copies + [c for _, c in p_copies]:
         copy.wait_send()
 
 
@@ -378,9 +392,15 @@
     both = pl.pallas_call(
         functools.partial(layer_kernel, n, cn),
         out_shape=jax.ShapeDtypeStruct((2, rows, width), bf16),
-        in_specs=[anywhere, vmem] + [anywhere] * 5 + [vmem] * 4,
+        in_specs=[anywhere] * 11,
         out_specs=vmem,
         scratch_shapes=[
+            pltpu.VMEM((1, cn * width), f32),
+            pltpu.VMEM(fwd_hi.shape, bf16),
+            pltpu.VMEM(fwd_lo.shape, bf16),
+            pltpu.VMEM(inv_hi.shape, bf16),
+            pltpu.VMEM(inv_lo.shape, bf16),
+            dma((5,)),
             pltpu.VMEM((cn, rows, width), bf16),
             pltpu.VMEM((cn, rows, width), bf16),
             pltpu.VMEM((3 * cn, width, width), bf16),

time: 54.1 us -> 50.3 us (0.930)
  Pallas kernels: 51.8 us -> 47.9 us
    pallas_call x1, Pallas kernels: 51.8 us -> 47.9 us  [fused_layer(): pl.pallas_call(functools.partial(layer_kernel, n, cn), out_shape=jax.Shap...]
where the time goes in v4:
time: 50.3 us; the launch traced here: 50.1 us
  Pallas kernels  47.9 us (95%)
  local copies, waits for them, and re-layouts  1.53 us (3%)
  between operations  0.64 us (1%)
    pallas_call x1, Pallas kernels, fused_layer(): pl.pallas_call(functools.partial(layer_kernel, n, cn), out_shape=jax.Shap...  47.9 us
    squeeze x1, local copies, waits for them, and re-layouts, fused_layer(): return (both[0], both[1])  1.53 us

profile of v4, /device:TPU:0, one launch (start us, length us, event | category | flops | bytes accessed | tf_op | source)
XLA Modules:
  0.0 50.1 jit_solution(17391851916420535859)
XLA Ops:
  0.6 47.9 %shard_map.122 = bf16[2,32,1024]{2,1,0:T(8,128)(2,1)} custom-call(bf16[32,1024]{1,0:T(8,128)(2,1)} %inputs.1, f32[1,4096]{1,0:T(1,128)} %bitcast.7, bf16[3,4096,1024]{2,1,0:T(8,128)(2,1)} %bitcast.6, bf16[1024,4096]{1,0:T(8,128)(2,1)} %w_out.1, bf16[256,2,1024]{2,1,0:T(2,128)(2,1)} %history.1, bf16[256,2,1024]{2,1,0:T(2,128)(2,1)} %filt_far.1, ...), custom_call_target="tpu_custom_call" | custom-call | tf_op jit(solution)/shard_map/pallas_call | solution.py:392
  48.6 1.5 %slice_bitcast_fusion = (bf16[32,1024]{1,0:T(8,128)(2,1)}, bf16[32,1024]{1,0:T(8,128)(2,1)}) fusion(bf16[2,32,1024]{2,1,0:T(8,128)(2,1)} %shard_map.122), kind=kLoop, calls=%fused_computation | loop fusion | bytes 262144 | tf_op jit(solution)/shard_map/squeeze | solution.py:436
